TPU v7x, 256 devices: a whole 4x4x8 slice. The times are simulated.
256 devices in a mesh: ep: 64 (over z, x, y_hi), tp: 4 (over y_lo, core).
Axes of the slice: x: 4, y: 4 (y_hi: 2, y_lo: 2; y = y_hi * 2 + y_lo), z: 8, core: 2. Of those that a mesh axis runs over, the one named last changes fastest.
Arguments:
- context: bfloat16 [8192, 4096], P('ep', 'tp'), may hold values from -6 to 6
- wo_proj: bfloat16 [4096, 4096], P('tp'), may hold values from -0.09375 to 0.09375
- residual: bfloat16 [8192, 4096], P(('ep', 'tp')), may hold values from -16 to 16
- norm_gain: bfloat16 [4096], replicated, may hold values from 0.25 to 1.75
- expert_ids: int32 [8192, 8], P(('ep', 'tp')), may hold values from 0 to 63, all different within a row; in each aligned block of 32 rows (0 to 31, 32 to 63, ...) at most 8 rows name the same one
- route_weights: float32 [8192, 8], P(('ep', 'tp')), may hold values from 0.1 to 1
- w_gate_up: bfloat16 [64, 2, 768, 4096], P('ep', None, 'tp'), may hold values from -0.09375 to 0.09375
- w_down: bfloat16 [64, 768, 4096], P('ep', 'tp'), may hold values from -0.21875 to 0.21875
Outputs:
- layer_out: bfloat16 [8192, 4096], P(('ep', 'tp'))
Inputs may be any that keep to these rules, and one draw needn't show every extreme that they name: `expert_ids`: within the routes of one device's 32 tokens no expert is named more than 8 times, a bound that some block reaches; a token names 8 different experts.
All inputs are finite; a program needn't handle non-finite values.
Results may differ from a plain program's by a relative error of at most 0.0085.
Values may be sent and summed in bfloat16 or wider, within the bound.
A program may use at most 128 MiB of HBM per device.

v0:
```python
import jax
import jax.numpy as jnp
from jax import lax
from jax.sharding import PartitionSpec as P


def local(context, wo_proj, residual, norm_gain, expert_ids, route_weights, w_gate_up, w_down):
    quarter_rows, model_width = residual.shape
    top_count = expert_ids.shape[1]
    exp_local = w_gate_up.shape[0]
    ep_size = lax.axis_size("ep")
    experts = exp_local * ep_size
    capacity = max(2, min(quarter_rows, 2 * quarter_rows * top_count // experts))
    gate_up_full = lax.all_gather(w_gate_up, "tp", axis=2, tiled=True)
    down_full = lax.all_gather(w_down, "tp", axis=1, tiled=True)
    attn = lax.psum_scatter(
        jnp.dot(context, wo_proj, preferred_element_type=jnp.float32),
        "tp",
        scatter_dimension=0,
        tiled=True,
    )
    hidden = residual.astype(jnp.float32) + attn
    inverse_rms = lax.rsqrt(jnp.mean(hidden * hidden, axis=1, keepdims=True) + 1e-06)
    normed = (hidden * inverse_rms * norm_gain.astype(jnp.float32)).astype(jnp.bfloat16)
    flat_ids = expert_ids.reshape(-1)
    onehot = (flat_ids[:, None] == jnp.arange(experts, dtype=jnp.int32)[None, :]).astype(jnp.int32)
    before = jnp.cumsum(onehot, axis=0, dtype=jnp.int32) - onehot
    position = jnp.sum(before * onehot, axis=1, dtype=jnp.int32)
    slot_ids = flat_ids * capacity + position
    slot_range = jnp.arange(experts * capacity, dtype=jnp.int32)
    selected = slot_range[:, None] == slot_ids[None, :]
    placement = jnp.any(
        selected.reshape(experts * capacity, quarter_rows, top_count), axis=2
    ).astype(jnp.bfloat16)
    send_rows = jnp.dot(placement, normed, preferred_element_type=jnp.float32).astype(jnp.bfloat16)
    send_rows = send_rows.reshape(ep_size, exp_local * capacity, model_width)
    received = lax.all_to_all(send_rows, "ep", split_axis=0, concat_axis=0, tiled=True)
    received = received.reshape(ep_size, exp_local, capacity, model_width)
    gate = jnp.einsum(
        "sjcd,jfd->sjcf", received, gate_up_full[:, 0], preferred_element_type=jnp.float32
    )
    up_proj = jnp.einsum(
        "sjcd,jfd->sjcf", received, gate_up_full[:, 1], preferred_element_type=jnp.float32
    )
    activated = (jax.nn.silu(gate) * up_proj).astype(jnp.bfloat16)
    expert_out = jnp.einsum(
        "sjcf,jfd->sjcd", activated, down_full, preferred_element_type=jnp.float32
    ).astype(jnp.bfloat16)
    returned = lax.all_to_all(
        expert_out.reshape(ep_size, exp_local * capacity, model_width),
        "ep",
        split_axis=0,
        concat_axis=0,
        tiled=True,
    )
    returned = returned.reshape(experts * capacity, model_width)
    token_slots = slot_ids.reshape(quarter_rows, top_count)
    mixture = jnp.zeros((quarter_rows, model_width), jnp.float32)
    for choice_index in range(top_count):
        picker = (slot_range[None, :] == token_slots[:, choice_index][:, None]).astype(jnp.bfloat16)
        picked = jnp.dot(picker, returned, preferred_element_type=jnp.float32)
        mixture = mixture + route_weights[:, choice_index : choice_index + 1] * picked
    return (hidden + mixture).astype(jnp.bfloat16)


def solution(mesh):
    in_specs = (
        P("ep", "tp"),
        P("tp", None),
        P(("ep", "tp"), None),
        P(),
        P(("ep", "tp"), None),
        P(("ep", "tp"), None),
        P("ep", None, "tp", None),
        P("ep", "tp", None),
    )
    out_specs = P(("ep", "tp"), None)
    return jax.shard_map(local, mesh=mesh, in_specs=in_specs, out_specs=out_specs, check_vma=False)
```

profile of v0, /device:TPU:1, one launch (start us, length us, event | category | flops | bytes accessed | tf_op | source)
XLA Modules:
  0.0 444.3 jit_solution(16430905282046604405)
XLA Ops:
  6.5 0.0 copy-start
  6.5 0.0 reduce-scatter.2.cloned.1.call-start
  6.5 0.9 copy-done
  7.5 5.9 %fusion.47 = f32[128,4096]{1,0:T(8,128)} fusion(bf16[128,1024]{1,0:T(8,128)(2,1)S(1)} %copy-done, bf16[1024,4096]{1,0:T(8,128)(2,1)} %param.9), kind=kOutput, calls=%fused_computation.94 | convolution fusion | flops 1073741824 | bytes 10747904 | tf_op jit(solution)/shard_map/dot_general | solution.py:17
  13.4 0.0 copy-start.4
  13.4 0.0 copy-start.3
  13.4 0.0 copy-start.2
  13.4 0.0 reduce-scatter.2.cloned.1.call-update
  13.5 0.0 all-gather.3.cloned.1.call-start
  13.5 0.7 all-gather.3.cloned.1.call-update
  14.2 0.0 all-gather.5.cloned.1.call-start
  14.3 0.7 all-gather.5.cloned.1.call-update
  14.9 0.0 copy-done.4
  15.0 0.1 copy.18
  15.0 0.1 eq.164
  15.1 0.1 eq.160
  15.2 0.0 copy-done.3
  15.3 0.6 reduce-window.6
  15.9 0.2 slice_reduce_fusion
  16.1 0.1 fusion.36
  16.2 0.1 reduce_sum.21
  16.3 0.2 fusion.31
  16.5 31.9 %reduce-scatter.2.cloned.1.call-done = f32[32,4096]{1,0:T(8,128)} async-done(((f32[128,4096]{1,0:T(8,128)}), f32[32,4096]{1,0:T(8,128)}) %reduce-scatter.2.cloned.1.call-update) | async-done | bytes 524304 | tf_op jit(solution)/shard_map/reduce_scatter | solution.py:16
  48.4 0.0 copy-done.2
  48.4 1.2 multiply_reduce_fusion
  49.6 2.4 fusion.7
  52.0 106.6 %all_to_all.10 = bf16[64,8,4096]{2,1,0:T(8,128)(2,1)} all-to-all(bf16[64,8,4096]{2,1,0:T(8,128)(2,1)S(1)} %fusion.7), channel_id=1, replica_groups=mesh['ep'=64,'tp'=4] {'ep'}, dimensions={0} | all-to-all | bytes 8388608 | tf_op jit(solution)/shard_map/all_to_all | solution.py:37
  158.6 53.6 %all-gather.3.cloned.1.call-done = bf16[1,2,768,4096]{3,2,1,0:T(8,128)(2,1)} async-done(((bf16[1,2,192,4096]{3,2,1,0:T(8,128)(2,1)}), bf16[1,2,768,4096]{3,2,1,0:T(8,128)(2,1)}) %all-gather.3.cloned.1.call-update) | async-done | bytes 12582928 | tf_op jit(solution)/shard_map/all_gather | solution.py:14
  212.2 7.1 %fusion.1 = f32[64,8,768]{2,1,0:T(8,128)S(1)} fusion(bf16[64,8,4096]{2,1,0:T(8,128)(2,1)} %all_to_all.10, bf16[1,2,768,4096]{3,2,1,0:T(8,128)(2,1)} %all-gather.3.cloned.1.call-done), kind=kOutput, calls=%fused_computation.3 | convolution fusion | flops 3221225472 | bytes 12058624 | tf_op jit(solution)/shard_map/sjcd,jfd->sjcf/dot_general | solution.py:39
  219.3 62.0 %all-gather.5.cloned.1.call-done = bf16[1,768,4096]{2,1,0:T(8,128)(2,1)} async-done(((bf16[1,192,4096]{2,1,0:T(8,128)(2,1)}), bf16[1,768,4096]{2,1,0:T(8,128)(2,1)}) %all-gather.5.cloned.1.call-update) | async-done | bytes 6291472 | tf_op jit(solution)/shard_map/all_gather | solution.py:15
  281.3 16.6 %fusion.4 = bf16[64,8,4096]{2,1,0:T(8,128)(2,1)} fusion(bf16[1,768,4096]{2,1,0:T(8,128)(2,1)} %all-gather.5.cloned.1.call-done, bf16[64,8,4096]{2,1,0:T(8,128)(2,1)} %all_to_all.10, bf16[1,2,768,4096]{3,2,1,0:T(8,128)(2,1)} %all-gather.3.cloned.1.call-done, f32[64,8,768]{2,1,0:T(8,128)S(1)} %fusion.1), kind=kOutput, calls=%fused_computation.6 | convolution fusion | flops 6446907392 | bytes 22544384 | tf_op jit(solution)/shard_map/sjcf,jfd->sjcd/dot_general | solution.py:46
  297.9 0.0 copy-start.5
  297.9 12.9 %all-to-all-start.1 = ((bf16[64,8,4096]{2,1,0:T(8,128)(2,1)}), bf16[64,8,4096]{2,1,0:T(8,128)(2,1)}, u32[]{:S(2)}, u32[]{:S(2)}) async-start(bf16[64,8,4096]{2,1,0:T(8,128)(2,1)} %fusion.4), calls=%async_computation.2 | async-start | bytes 8388608 | tf_op jit(solution)/shard_map/all_to_all | solution.py:49
  310.8 0.3 slice_reduce_fusion.1
  311.2 0.0 copy-done.5
  311.2 101.4 %all-to-all-done.1 = bf16[64,8,4096]{2,1,0:T(8,128)(2,1)} async-done(((bf16[64,8,4096]{2,1,0:T(8,128)(2,1)}), bf16[64,8,4096]{2,1,0:T(8,128)(2,1)}, u32[]{:S(2)}, u32[]{:S(2)}) %all-to-all-start.1) | async-done | bytes 4194336 | tf_op jit(solution)/shard_map/all_to_all | solution.py:49
  412.5 3.0 convolution_multiply_fusion.7
  415.6 3.0 fusion.15
  418.6 3.0 fusion.14
  421.7 3.0 fusion.13
  424.7 3.0 fusion.12
  427.8 0.0 copy-start.1
  427.8 3.1 fusion.11
  430.9 3.0 fusion.10
  434.0 0.0 copy-done.1
  434.0 3.8 fusion.16
  (7 shorter events, 0.1 us)
Async XLA Ops:
  6.5 1.0 copy-start
  6.5 41.9 %reduce-scatter.2.cloned.1.call-start = ((), (), s32[]{:S(2)}) async-start(), calls=%async_computation.3 | async-start | bytes 2621440 | tf_op jit(solution)/shard_map/reduce_scatter | solution.py:16
  13.4 1.5 copy-start.4
  13.4 1.8 copy-start.3
  13.4 35.0 %copy-start.2 = (bf16[32,4096]{1,0:T(8,128)(2,1)S(1)}, bf16[32,4096]{1,0:T(8,128)(2,1)}, u32[]{:S(2)}) copy-start(bf16[32,4096]{1,0:T(8,128)(2,1)} %param.10) | copy-start | bytes 786436
  13.5 198.7 %all-gather.3.cloned.1.call-start = ((), (), s32[]{:S(2)}) async-start(), calls=%async_computation.4 | async-start | bytes 15728640 | tf_op jit(solution)/shard_map/all_gather | solution.py:14
  14.2 267.1 %all-gather.5.cloned.1.call-start = ((), (), s32[]{:S(2)}) async-start(), calls=%async_computation.5 | async-start | bytes 7864320 | tf_op jit(solution)/shard_map/all_gather | solution.py:15
  297.9 13.2 %copy-start.5 = (f32[32,8]{0,1:T(8,128)S(1)}, f32[32,8]{0,1:T(8,128)}, u32[]{:S(2)}) copy-start(f32[32,8]{0,1:T(8,128)} %param.13) | copy-start | bytes 3076
  297.9 114.6 %all-to-all-start.1 = ((bf16[64,8,4096]{2,1,0:T(8,128)(2,1)}), bf16[64,8,4096]{2,1,0:T(8,128)(2,1)}, u32[]{:S(2)}, u32[]{:S(2)}) async-start(bf16[64,8,4096]{2,1,0:T(8,128)(2,1)} %fusion.4), calls=%async_computation.2 | async-start | bytes 8388608 | tf_op jit(solution)/shard_map/all_to_all | solution.py:49
  427.8 6.2 %copy-start.1 = (f32[32,4096]{1,0:T(8,128)S(1)}, f32[32,4096]{1,0:T(8,128)}, u32[]{:S(2)}) copy-start(f32[32,4096]{1,0:T(8,128)} %reduce-scatter.2.cloned.1.call-done) | copy-start | bytes 1572868
Sparse Core Ops, SparseCore 0:
  13.6 34.7 reduce-scatter.1
  50.2 161.9 all-gather.2
  214.0 67.2 all-gather.4
where the time goes:
time: 445 us; the launch traced here: 444 us
  waiting for transfers between devices  250 us (56%)
  blocking collectives  107 us (24%)
  matrix products  57.2 us (13%)
  between operations  13.3 us (3%)
  starting transfers between devices  13 us (3%)
    all_to_all x1, blocking collectives, local(): lax.all_to_all(send_rows, 'ep', split_axis=0, concat_axis=0, tiled=True)  107 us
    all_to_all x1, waiting for transfers between devices, local(): lax.all_to_all(expert_out.reshape(ep_size, exp_local * capacity, model_wi...  101 us
    all_gather x1, waiting for transfers between devices, local(): down_full = lax.all_gather(w_down, 'tp', axis=1, tiled=True)  62 us
    all_gather x1, waiting for transfers between devices, local(): gate_up_full = lax.all_gather(w_gate_up, 'tp', axis=2, tiled=True)  53.6 us
    reduce_scatter x1, waiting for transfers between devices, local(): lax.psum_scatter(jnp.dot(context, wo_proj, preferred_element_type=jnp.flo...  31.9 us
    dot_general x8, matrix products, local(): picked = jnp.dot(picker, returned, preferred_element_type=jnp.float32)  25.1 us
    dot_general x1, matrix products, local(): jnp.einsum('sjcf,jfd->sjcd', activated, down_full, preferred_element_type...  16.6 us
    all_to_all x1, starting transfers between devices, local(): lax.all_to_all(expert_out.reshape(ep_size, exp_local * capacity, model_wi...  12.9 us
  transfers between devices with their start and end apart: 4, of which 4 were waited for; matrix products, arithmetic and copies ran while one was open for 3% of the time, Pallas kernels for 0%

commit v1 on v0

--- a/solution.py
+++ b/solution.py
@@ -12,7 +12,9 @@
     experts = exp_local * ep_size
     capacity = max(2, min(quarter_rows, 2 * quarter_rows * top_count // experts))
     gate_up_full = lax.all_gather(w_gate_up, "tp", axis=2, tiled=True)
-    down_full = lax.all_gather(w_down, "tp", axis=1, tiled=True)
+    down_full = jnp.concatenate(
+        lax.all_to_all(jnp.stack([w_down] * lax.axis_size("tp")), "tp", 0, 0), axis=1
+    )
     attn = lax.psum_scatter(
         jnp.dot(context, wo_proj, preferred_element_type=jnp.float32),
         "tp",

time: 445 us -> 437 us (0.982)
  waiting for transfers between devices: 250 us -> 227 us
  starting transfers between devices: 13 us -> 21.8 us
    all_gather x1 -> x0, waiting for transfers between devices: 62 us -> none  [local(): down_full = lax.all_gather(w_down, 'tp', axis=1, tiled=True)]
    all_gather x1, waiting for transfers between devices: 53.6 us -> 78.9 us  [local(): gate_up_full = lax.all_gather(w_gate_up, 'tp', axis=2, tiled=True)]
    all_to_all x0 -> x1, waiting for transfers between devices: none -> 22.2 us  [local(): lax.all_to_all(jnp.stack([w_down] * lax.axis_size('tp')), 'tp', 0, 0)]
    all_to_all x0 -> x1, starting transfers between devices: none -> 9.29 us  [local(): lax.all_to_all(jnp.stack([w_down] * lax.axis_size('tp')), 'tp', 0, 0)]
    all_to_all x1, waiting for transfers between devices: 101 us -> 93 us  [local(): lax.all_to_all(expert_out.reshape(ep_size, exp_local * capacity, model_wi...]
  transfers between devices with their start and end apart: 4 -> 4, of which waited for: 4 -> 4; matrix products, arithmetic and copies ran while one was open for 3% -> 4% of each run, Pallas kernels for 0% -> 0%
where the time goes in v1:
time: 437 us; the launch traced here: 434 us
  waiting for transfers between devices  227 us (52%)
  blocking collectives  107 us (24%)
  matrix products  57.3 us (13%)
  starting transfers between devices  21.8 us (5%)
  between operations  13.6 us (3%)
  local copies, waits for them, and re-layouts  5.19 us (1%)
    all_to_all x1, blocking collectives, local(): lax.all_to_all(send_rows, 'ep', split_axis=0, concat_axis=0, tiled=True)  107 us
    all_to_all x1, waiting for transfers between devices, local(): lax.all_to_all(expert_out.reshape(ep_size, exp_local * capacity, model_wi...  93 us
    all_gather x1, waiting for transfers between devices, local(): gate_up_full = lax.all_gather(w_gate_up, 'tp', axis=2, tiled=True)  78.9 us
    reduce_scatter x1, waiting for transfers between devices, local(): lax.psum_scatter(jnp.dot(context, wo_proj, preferred_element_type=jnp.flo...  32.6 us
    dot_general x8, matrix products, local(): picked = jnp.dot(picker, returned, preferred_element_type=jnp.float32)  25.1 us
    all_to_all x1, waiting for transfers between devices, local(): lax.all_to_all(jnp.stack([w_down] * lax.axis_size('tp')), 'tp', 0, 0)  22.2 us
    dot_general x1, matrix products, local(): jnp.einsum('sjcf,jfd->sjcd', activated, down_full, preferred_element_type...  16.6 us
    all_to_all x1, starting transfers between devices, local(): lax.all_to_all(expert_out.reshape(ep_size, exp_local * capacity, model_wi...  12.5 us
  transfers between devices with their start and end apart: 4, of which 4 were waited for; matrix products, arithmetic and copies ran while one was open for 4% of the time, Pallas kernels for 0%

profile of v1, /device:TPU:1, one launch (start us, length us, event | category | flops | bytes accessed | tf_op | source)
XLA Modules:
  0.0 434.1 jit_solution(16740358715680958488)
XLA Ops:
  6.5 0.0 copy-start
  6.5 0.0 reduce-scatter.2.cloned.1.call-start
  6.5 0.9 copy-done
  7.5 6.0 %fusion.41 = f32[128,4096]{1,0:T(8,128)} fusion(bf16[128,1024]{1,0:T(8,128)(2,1)S(1)} %copy-done, bf16[1024,4096]{1,0:T(8,128)(2,1)} %param.9), kind=kOutput, calls=%fused_computation.91 | convolution fusion | flops 1073741824 | bytes 10747904 | tf_op jit(solution)/shard_map/dot_general | solution.py:19
  13.5 0.0 copy-start.5
  13.5 0.0 copy-start.4
  13.5 0.0 copy-start.2
  13.5 0.0 reduce-scatter.2.cloned.1.call-update
  13.5 0.0 all-gather.2.cloned.1.call-start
  13.6 0.7 all-gather.2.cloned.1.call-update
  14.3 0.0 copy-done.5
  14.3 0.1 copy.22
  14.4 0.1 eq.160
  14.5 0.1 eq.164
  14.6 0.6 reduce-window.6
  15.2 0.2 slice_reduce_fusion
  15.4 0.1 fusion.30
  15.5 0.1 reduce_sum.21
  15.6 0.0 copy-done.4
  15.6 0.2 fusion.25
  15.9 32.6 %reduce-scatter.2.cloned.1.call-done = f32[32,4096]{1,0:T(8,128)} async-done(((f32[128,4096]{1,0:T(8,128)}), f32[32,4096]{1,0:T(8,128)}) %reduce-scatter.2.cloned.1.call-update) | async-done | bytes 524304 | tf_op jit(solution)/shard_map/reduce_scatter | solution.py:18
  48.5 0.0 copy-done.2
  48.5 1.2 multiply_reduce_fusion
  49.7 2.4 fusion.2
  52.1 0.0 copy-start.3
  52.1 106.7 %all_to_all.15 = bf16[64,8,4096]{2,1,0:T(8,128)(2,1)} all-to-all(bf16[64,8,4096]{2,1,0:T(8,128)(2,1)S(1)} %fusion.2), channel_id=1, replica_groups=mesh['ep'=64,'tp'=4] {'ep'}, dimensions={0} | all-to-all | bytes 8388608 | tf_op jit(solution)/shard_map/all_to_all | solution.py:39
  158.8 0.0 copy-done.3
  158.8 3.4 stack.2
  162.2 9.3 %all-to-all-start.1 = ((bf16[4,1,192,4096]{3,2,1,0:T(8,128)(2,1)}), bf16[4,1,192,4096]{3,2,1,0:T(8,128)(2,1)}, u32[]{:S(2)}, u32[]{:S(2)}) async-start(bf16[4,1,192,4096]{3,2,1,0:T(8,128)(2,1)} %stack.2), calls=%async_computation.2 | async-start | bytes 12582912 | tf_op jit(solution)/shard_map/all_to_all | solution.py:16
  171.4 78.9 %all-gather.2.cloned.1.call-done = bf16[1,2,768,4096]{3,2,1,0:T(8,128)(2,1)} async-done(((bf16[1,2,192,4096]{3,2,1,0:T(8,128)(2,1)}), bf16[1,2,768,4096]{3,2,1,0:T(8,128)(2,1)}) %all-gather.2.cloned.1.call-update) | async-done | bytes 12582928 | tf_op jit(solution)/shard_map/all_gather | solution.py:14
  250.4 7.1 %fusion.1 = f32[64,8,768]{2,1,0:T(8,128)S(1)} fusion(bf16[64,8,4096]{2,1,0:T(8,128)(2,1)} %all_to_all.15, bf16[1,2,768,4096]{3,2,1,0:T(8,128)(2,1)} %all-gather.2.cloned.1.call-done), kind=kOutput, calls=%fused_computation.3 | convolution fusion | flops 3221225472 | bytes 12058624 | tf_op jit(solution)/shard_map/sjcd,jfd->sjcf/dot_general | solution.py:41
  257.5 22.2 %all-to-all-done.1 = bf16[4,1,192,4096]{3,2,1,0:T(8,128)(2,1)} async-done(((bf16[4,1,192,4096]{3,2,1,0:T(8,128)(2,1)}), bf16[4,1,192,4096]{3,2,1,0:T(8,128)(2,1)}, u32[]{:S(2)}, u32[]{:S(2)}) %all-to-all-start.1) | async-done | bytes 6291488 | tf_op jit(solution)/shard_map/all_to_all | solution.py:16
  279.6 16.6 %convolution_convert_fusion = bf16[64,8,4096]{2,1,0:T(8,128)(2,1)} fusion(bf16[768,4096,1]{1,0,2:T(8,128)(2,1)} %bitcast.18, bf16[64,8,4096]{2,1,0:T(8,128)(2,1)} %all_to_all.15, bf16[1,2,768,4096]{3,2,1,0:T(8,128)(2,1)} %all-gather.2.cloned.1.call-done, f32[64,8,768]{2,1,0:T(8,128)S(1)} %fusion.1), kind=kOutput, calls=%fused_computation.4 | convolution fusion | flops 6446907392 | bytes 22544384 | tf_op jit(solution)/shard_map/sjcf,jfd->sjcd/dot_general | solution.py:48
  296.3 0.0 copy-start.6
  296.3 12.5 %all-to-all-start.2 = ((bf16[64,8,4096]{2,1,0:T(8,128)(2,1)}), bf16[64,8,4096]{2,1,0:T(8,128)(2,1)}, u32[]{:S(2)}, u32[]{:S(2)}) async-start(bf16[64,8,4096]{2,1,0:T(8,128)(2,1)} %convolution_convert_fusion), calls=%async_computation.3 | async-start | bytes 8388608 | tf_op jit(solution)/shard_map/all_to_all | solution.py:51
  308.8 0.3 slice_reduce_fusion.1
  309.1 0.0 copy-done.6
  309.1 93.0 %all-to-all-done.2 = bf16[64,8,4096]{2,1,0:T(8,128)(2,1)} async-done(((bf16[64,8,4096]{2,1,0:T(8,128)(2,1)}), bf16[64,8,4096]{2,1,0:T(8,128)(2,1)}, u32[]{:S(2)}, u32[]{:S(2)}) %all-to-all-start.2) | async-done | bytes 4194336 | tf_op jit(solution)/shard_map/all_to_all | solution.py:51
  402.1 3.0 convolution_multiply_fusion.7
  405.1 3.0 fusion.10
  408.2 3.0 fusion.9
  411.2 3.0 fusion.8
  414.3 3.0 fusion.7
  417.3 0.0 copy-start.1
  417.3 3.1 fusion.6
  420.4 3.0 fusion.5
  423.5 0.0 copy-done.1
  423.5 3.8 fusion.11
  (7 shorter events, 0.1 us)
Async XLA Ops:
  6.5 1.0 copy-start
  6.5 41.9 %reduce-scatter.2.cloned.1.call-start = ((), (), s32[]{:S(2)}) async-start(), calls=%async_computation.4 | async-start | bytes 2621440 | tf_op jit(solution)/shard_map/reduce_scatter | solution.py:18
  13.5 0.8 copy-start.5
  13.5 2.1 copy-start.4
  13.5 35.0 %copy-start.2 = (bf16[32,4096]{1,0:T(8,128)(2,1)S(1)}, bf16[32,4096]{1,0:T(8,128)(2,1)}, u32[]{:S(2)}) copy-start(bf16[32,4096]{1,0:T(8,128)(2,1)} %param.10) | copy-start | bytes 786436
  13.5 236.9 %all-gather.2.cloned.1.call-start = ((), (), s32[]{:S(2)}) async-start(), calls=%async_computation.5 | async-start | bytes 15728640 | tf_op jit(solution)/shard_map/all_gather | solution.py:14
  52.1 106.7 %copy-start.3 = (bf16[1,192,4096]{2,1,0:T(8,128)(2,1)S(1)}, bf16[1,192,4096]{2,1,0:T(8,128)(2,1)}, u32[]{:S(2)}) copy-start(bf16[1,192,4096]{2,1,0:T(8,128)(2,1)} %param.15) | copy-start | bytes 4718596
  162.2 117.5 %all-to-all-start.1 = ((bf16[4,1,192,4096]{3,2,1,0:T(8,128)(2,1)}), bf16[4,1,192,4096]{3,2,1,0:T(8,128)(2,1)}, u32[]{:S(2)}, u32[]{:S(2)}) async-start(bf16[4,1,192,4096]{3,2,1,0:T(8,128)(2,1)} %stack.2), calls=%async_computation.2 | async-start | bytes 12582912 | tf_op jit(solution)/shard_map/all_to_all | solution.py:16
  296.3 12.8 %copy-start.6 = (f32[32,8]{0,1:T(8,128)S(1)}, f32[32,8]{0,1:T(8,128)}, u32[]{:S(2)}) copy-start(f32[32,8]{0,1:T(8,128)} %param.13) | copy-start | bytes 3076
  296.3 105.8 %all-to-all-start.2 = ((bf16[64,8,4096]{2,1,0:T(8,128)(2,1)}), bf16[64,8,4096]{2,1,0:T(8,128)(2,1)}, u32[]{:S(2)}, u32[]{:S(2)}) async-start(bf16[64,8,4096]{2,1,0:T(8,128)(2,1)} %convolution_convert_fusion), calls=%async_computation.3 | async-start | bytes 8388608 | tf_op jit(solution)/shard_map/all_to_all | solution.py:51
  417.3 6.2 %copy-start.1 = (f32[32,4096]{1,0:T(8,128)S(1)}, f32[32,4096]{1,0:T(8,128)}, u32[]{:S(2)}) copy-start(f32[32,4096]{1,0:T(8,128)} %reduce-scatter.2.cloned.1.call-done) | copy-start | bytes 1572868
Sparse Core Ops, SparseCore 0:
  13.6 34.7 reduce-scatter.1
  50.3 200.0 all-gather.1
